TPU v7x, 32 devices: a whole 2x2x4 slice. The times are simulated.
32 devices in a mesh: seq: 4 (over x, core), wshard: 8 (over z, y).
Axes of the slice: x: 2, y: 2, z: 4, core: 2. Of those that a mesh axis runs over, the one named last changes fastest.
Arguments:
- tokens: bfloat16 [8, 2048, 2048], P('wshard', 'seq'), may hold values from -6 to 6
- cotangent: bfloat16 [8, 2048, 2048], P('wshard', 'seq'), may hold values from -6 to 6
- order: int32 [8, 2048], P('wshard'), may hold values from 0 to 2047, each once within a row
- sequence_lengths: int32 [8, 2], P('wshard'), may hold values from 1024 to 1024, as said below
- adapter_per_sequence: int32 [8, 2], P('wshard'), may hold values from 0 to 7
- first_norm_scale: bfloat16 [2048], replicated, may hold values from 0.5 to 1.5
- first_norm_bias: bfloat16 [2048], replicated, may hold values from -1.75 to 1.75
- query_key_value_weight: bfloat16 [2048, 6144], P('wshard'), may hold values from -0.125 to 0.125
- query_key_value_bias: bfloat16 [6144], replicated, may hold values from -1.75 to 1.75
- attention_output_weight: bfloat16 [2048, 2048], P('wshard'), may hold values from -0.5 to 0.5
- second_norm_scale: bfloat16 [2048], replicated, may hold values from 0.5 to 1.5
- second_norm_bias: bfloat16 [2048], replicated, may hold values from -1.75 to 1.75
- gate_up_weight: bfloat16 [2048, 11264], P('wshard'), may hold values from -0.125 to 0.125
- down_weight: bfloat16 [5632, 2048], P('wshard'), may hold values from -0.078125 to 0.078125
- first_factors_width: bfloat16 [6, 2048, 128], replicated, may hold values from -0.125 to 0.125
- first_factors_hidden: bfloat16 [5632, 128], replicated, may hold values from -0.078125 to 0.078125
- second_factors_width: bfloat16 [5, 2048, 128], replicated, may hold values from -0.75 to 0.75
- second_factors_hidden: bfloat16 [2, 5632, 128], replicated, may hold values from -0.75 to 0.75
Outputs:
- mixed: bfloat16 [8, 2048, 2048], P('wshard', 'seq')
- grad_tokens: bfloat16 [8, 2048, 2048], P('wshard', 'seq')
- grad_lora_in_d: float32 [6, 2048, 128], P(None, None, ('seq', 'wshard'))
- grad_lora_in_ff: float32 [5632, 128], P(None, ('seq', 'wshard'))
- grad_lora_out_d: float32 [5, 2048, 128], P(None, None, ('seq', 'wshard'))
- grad_lora_out_ff: float32 [2, 5632, 128], P(None, None, ('seq', 'wshard'))
Inputs may be any that keep to these rules, and one draw needn't show every extreme that they name: Each row of order is a permutation. `sequence_lengths`: each row sums to 2048; every length is at least 1024.
All inputs are finite; a program needn't handle non-finite values.
Results may differ from a plain program's by a relative error of at most 0.015.
Values may be sent and summed in bfloat16 or wider, within the bound.
No kernel may reach another device: no remote copies, remote signals or barrier semaphores. Data moves between devices by JAX's collectives and lax.ppermute only.
A program may use at most 384 MiB of HBM per device.

v0:
```python
import math

import jax
import jax.numpy as jnp
from jax import lax
from jax.sharding import PartitionSpec as P

MODEL_WIDTH = 2048
HEAD_DIM = 64
ROT = 16
HIDDEN_UNITS = 5632
ADAPTER_RANK = 16
ADAPTER_COUNT = 8


NORM_EPS = 1e-05
NEG_FILL = -1e30
ROPE_BASE = 10000.0
CONTRACT_FINAL = (((1,), (1,)), ((), ()))
CONTRACT_FIRST = (((0,), (0,)), ((), ()))


def token_info(order_row, lengths, idents):
    seq_count = lengths.shape[0]
    seq_ends = jnp.cumsum(lengths)
    starts = seq_ends - lengths
    segment = jnp.sum((order_row[:, None] >= seq_ends[None, :]).astype(jnp.int32), axis=1)
    onehot = segment[:, None] == jnp.arange(seq_count, dtype=jnp.int32)[None, :]
    seg_begin = jnp.sum(jnp.where(onehot, starts[None, :], 0), axis=1)
    adapter = jnp.sum(jnp.where(onehot, idents[None, :], 0), axis=1)
    position = (order_row - seg_begin).astype(jnp.float32)
    columns = jnp.arange(ADAPTER_COUNT * ADAPTER_RANK, dtype=jnp.int32) // ADAPTER_RANK
    select_adapter = (columns[None, :] == adapter[:, None]).astype(jnp.float32)
    return (segment, position, select_adapter)


def rope_tables(position):
    half_rot = ROT // 2
    frequency = jnp.exp(
        jnp.arange(half_rot, dtype=jnp.float32) * (-2.0 * math.log(ROPE_BASE) / ROT)
    )
    angles = position[:, None] * frequency[None, :]
    return (jnp.cos(angles), jnp.sin(angles))


def rotate(values, cosine, sine_tab):
    half_rot = ROT // 2
    first_half = values[..., :half_rot]
    second_half = values[..., half_rot:ROT]
    cos_wide = cosine[:, None, :]
    sin_wide = sine_tab[:, None, :]
    return jnp.concatenate(
        [
            first_half * cos_wide - second_half * sin_wide,
            second_half * cos_wide + first_half * sin_wide,
            values[..., ROT:],
        ],
        axis=-1,
    )


def unrotate(grads, cosine, sine_tab):
    half_rot = ROT // 2
    first_half = grads[..., :half_rot]
    second_half = grads[..., half_rot:ROT]
    cos_wide = cosine[:, None, :]
    sin_wide = sine_tab[:, None, :]
    return jnp.concatenate(
        [
            first_half * cos_wide + second_half * sin_wide,
            second_half * cos_wide - first_half * sin_wide,
            grads[..., ROT:],
        ],
        axis=-1,
    )


def norm_forward(values, norm_gain, norm_shift):
    center = values - jnp.mean(values, axis=-1, keepdims=True)
    spread = jnp.mean(center * center, axis=-1, keepdims=True)
    inverse = lax.rsqrt(spread + NORM_EPS)
    scaled = center * inverse
    return (scaled * norm_gain + norm_shift, scaled, inverse)


def norm_backward(grad_in, scaled, inverse, norm_gain):
    dscaled = grad_in * norm_gain
    return inverse * (
        dscaled
        - jnp.mean(dscaled, axis=-1, keepdims=True)
        - scaled * jnp.mean(dscaled * scaled, axis=-1, keepdims=True)
    )


def low_rank_inner(product_operand, low_rank_first, select_adapter):
    return (
        select_adapter
        * jnp.dot(product_operand, low_rank_first, preferred_element_type=jnp.float32)
    ).astype(jnp.bfloat16)


def apply_low_rank(inner_product, low_rank_second):
    return lax.dot_general(
        inner_product, low_rank_second, CONTRACT_FINAL, preferred_element_type=jnp.float32
    )


def low_rank_backward(
    product_operand, row_gradients, inner_product, low_rank_first, low_rank_second, select_adapter
):
    output_factor_gradient = lax.dot_general(
        row_gradients, inner_product, CONTRACT_FIRST, preferred_element_type=jnp.float32
    )
    reverse_result = (
        select_adapter * jnp.dot(row_gradients, low_rank_second, preferred_element_type=jnp.float32)
    ).astype(jnp.bfloat16)
    input_factor_gradient = lax.dot_general(
        product_operand, reverse_result, CONTRACT_FIRST, preferred_element_type=jnp.float32
    )
    input_gradient = lax.dot_general(
        reverse_result, low_rank_first, CONTRACT_FINAL, preferred_element_type=jnp.float32
    )
    return (input_factor_gradient, output_factor_gradient, input_gradient)


def row_fold(product_operand, weight_rows):
    return jnp.dot(product_operand, weight_rows, preferred_element_type=jnp.float32)


def col_product(row_gradients, weight_rows):
    return lax.dot_general(
        row_gradients, weight_rows, CONTRACT_FINAL, preferred_element_type=jnp.float32
    )


def masked_scores(rows_q, k_rot, seg_q, ord_q, segment, order_row, score_scale):
    scores = (
        jnp.einsum("qhd,khd->hqk", rows_q, k_rot, preferred_element_type=jnp.float32) * score_scale
    )
    allowed = (seg_q[:, None] == segment[None, :]) & (order_row[None, :] <= ord_q[:, None])
    return jnp.where(allowed[None], scores, NEG_FILL)


def local(
    tokens,
    cotangent,
    order,
    sequence_lengths,
    adapter_per_sequence,
    first_norm_scale,
    first_norm_bias,
    query_key_value_weight,
    query_key_value_bias,
    attention_output_weight,
    second_norm_scale,
    second_norm_bias,
    gate_up_weight,
    down_weight,
    first_factors_width,
    first_factors_hidden,
    second_factors_width,
    second_factors_hidden,
):
    f32 = jnp.float32
    to_brainfloat = jnp.bfloat16
    rows_dev = tokens.shape[1]
    order_row = order[0]
    group_rows = order_row.shape[0]
    segment, position, select_all = token_info(
        order_row, sequence_lengths[0], adapter_per_sequence[0]
    )
    row_base = lax.axis_index("seq") * rows_dev
    select_adapter = lax.dynamic_slice_in_dim(select_all, row_base, rows_dev, 0)
    input_rows = tokens[0].astype(f32)
    gain_one = first_norm_scale.astype(f32)
    gain_two = second_norm_scale.astype(f32)
    normed, scaled_one, inverse_one = norm_forward(
        input_rows, gain_one, first_norm_bias.astype(f32)
    )
    normalized_brain = normed.astype(to_brainfloat)
    joint_qkv = row_fold(
        normalized_brain, lax.all_gather(query_key_value_weight, "wshard", axis=0, tiled=True)
    )
    joint_qkv = joint_qkv + query_key_value_bias.astype(f32)
    query_key_value_inner = [
        low_rank_inner(normalized_brain, first_factors_width[projection_index], select_adapter)
        for projection_index in range(3)
    ]
    proj_tok = [
        (
            joint_qkv[:, projection_index * MODEL_WIDTH : (projection_index + 1) * MODEL_WIDTH]
            + apply_low_rank(
                query_key_value_inner[projection_index], second_factors_width[projection_index]
            )
        ).astype(to_brainfloat)
        for projection_index in range(3)
    ]
    q_heads, k_heads, v_heads = (
        lax.all_to_all(proj_tok[0], "seq", split_axis=1, concat_axis=0, tiled=True),
        lax.all_to_all(proj_tok[1], "seq", split_axis=1, concat_axis=0, tiled=True),
        lax.all_to_all(proj_tok[2], "seq", split_axis=1, concat_axis=0, tiled=True),
    )
    head_count = q_heads.shape[1] // HEAD_DIM
    heads_shape = (group_rows, head_count, HEAD_DIM)
    cosine, sine_tab = rope_tables(position)
    q_rot = rotate(q_heads.reshape(heads_shape).astype(f32), cosine, sine_tab).astype(to_brainfloat)
    k_rot = rotate(k_heads.reshape(heads_shape).astype(f32), cosine, sine_tab).astype(to_brainfloat)
    v_all = v_heads.reshape(heads_shape)
    qblock = min(512, group_rows)
    block_count = group_rows // qblock
    score_scale = 1.0 / math.sqrt(HEAD_DIM)

    def attend(block_idx):
        row_start = block_idx * qblock
        rows_q = lax.dynamic_slice_in_dim(q_rot, row_start, qblock, 0)
        seg_q = lax.dynamic_slice_in_dim(segment, row_start, qblock, 0)
        ord_q = lax.dynamic_slice_in_dim(order_row, row_start, qblock, 0)
        scores = masked_scores(rows_q, k_rot, seg_q, ord_q, segment, order_row, score_scale)
        row_max = jnp.max(scores, axis=-1, keepdims=True)
        expo = jnp.exp(scores - row_max)
        row_total = jnp.sum(expo, axis=-1, keepdims=True)
        probs = expo / row_total
        block_out = jnp.einsum(
            "hqk,khd->qhd", probs.astype(to_brainfloat), v_all, preferred_element_type=f32
        )
        return (block_out, (row_max + jnp.log(row_total))[..., 0])

    attended, log_norms = lax.map(attend, jnp.arange(block_count, dtype=jnp.int32))
    attended = attended.reshape(group_rows, head_count * HEAD_DIM).astype(to_brainfloat)
    attention_tokens = lax.all_to_all(attended, "seq", split_axis=0, concat_axis=1, tiled=True)
    output_inner_rows = low_rank_inner(attention_tokens, first_factors_width[3], select_adapter)
    residual_branch = row_fold(
        attention_tokens, lax.all_gather(attention_output_weight, "wshard", axis=0, tiled=True)
    )
    incoming_hidden = (
        input_rows + residual_branch + apply_low_rank(output_inner_rows, second_factors_width[3])
    )
    normed_two, scaled_two, inverse_two = norm_forward(
        incoming_hidden, gain_two, second_norm_bias.astype(f32)
    )
    normalized_second_brain = normed_two.astype(to_brainfloat)
    joint_gate_up = row_fold(
        normalized_second_brain, lax.all_gather(gate_up_weight, "wshard", axis=0, tiled=True)
    )
    gate_inner_rows = low_rank_inner(
        normalized_second_brain, first_factors_width[4], select_adapter
    )
    up_inner_rows = low_rank_inner(normalized_second_brain, first_factors_width[5], select_adapter)
    gate_activation = joint_gate_up[:, :HIDDEN_UNITS] + apply_low_rank(
        gate_inner_rows, second_factors_hidden[0]
    )
    up_activation = joint_gate_up[:, HIDDEN_UNITS:] + apply_low_rank(
        up_inner_rows, second_factors_hidden[1]
    )
    sigmoid_gate = jax.nn.sigmoid(gate_activation)
    silu_gate = gate_activation * sigmoid_gate
    hidden_state = (silu_gate * up_activation).astype(to_brainfloat)
    down_inner_rows = low_rank_inner(hidden_state, first_factors_hidden, select_adapter)
    residual_branch_second = row_fold(
        hidden_state, lax.all_gather(down_weight, "wshard", axis=0, tiled=True)
    )
    mixed = (
        incoming_hidden
        + residual_branch_second
        + apply_low_rank(down_inner_rows, second_factors_width[4])
    ).astype(to_brainfloat)
    mixed_gradient = cotangent[0]
    grad_top = mixed_gradient.astype(f32)
    down_first_factor, down_second_factor, down_reverse = low_rank_backward(
        hidden_state,
        mixed_gradient,
        down_inner_rows,
        first_factors_hidden,
        second_factors_width[4],
        select_adapter,
    )
    d_hidden = col_product(
        mixed_gradient, lax.all_gather(down_weight, "wshard", axis=0, tiled=True)
    )
    d_hidden = d_hidden + down_reverse
    gate_gradient = (
        d_hidden * up_activation * (sigmoid_gate * (1.0 + gate_activation * (1.0 - sigmoid_gate)))
    ).astype(to_brainfloat)
    up_gradient = (d_hidden * silu_gate).astype(to_brainfloat)
    gate_first_factor, gate_second_factor, gate_reverse = low_rank_backward(
        normalized_second_brain,
        gate_gradient,
        gate_inner_rows,
        first_factors_width[4],
        second_factors_hidden[0],
        select_adapter,
    )
    up_first_factor, up_second_factor, up_reverse = low_rank_backward(
        normalized_second_brain,
        up_gradient,
        up_inner_rows,
        first_factors_width[5],
        second_factors_hidden[1],
        select_adapter,
    )
    grad_gu = jnp.concatenate([gate_gradient, up_gradient], axis=1)
    d_normed_two = col_product(
        grad_gu, lax.all_gather(gate_up_weight, "wshard", axis=0, tiled=True)
    )
    d_normed_two = d_normed_two + gate_reverse + up_reverse
    d_hidden_in = grad_top + norm_backward(d_normed_two, scaled_two, inverse_two, gain_two)
    branch_gradient = d_hidden_in.astype(to_brainfloat)
    output_first_factor, output_second_factor, output_reverse = low_rank_backward(
        attention_tokens,
        branch_gradient,
        output_inner_rows,
        first_factors_width[3],
        second_factors_width[3],
        select_adapter,
    )
    d_att = col_product(
        branch_gradient, lax.all_gather(attention_output_weight, "wshard", axis=0, tiled=True)
    )
    d_att = (d_att + output_reverse).astype(to_brainfloat)
    d_heads = lax.all_to_all(d_att, "seq", split_axis=1, concat_axis=0, tiled=True).reshape(
        heads_shape
    )

    def attend_back(carry_in, block_idx):
        key_acc, value_acc = carry_in
        row_start = block_idx * qblock
        rows_q = lax.dynamic_slice_in_dim(q_rot, row_start, qblock, 0)
        seg_q = lax.dynamic_slice_in_dim(segment, row_start, qblock, 0)
        ord_q = lax.dynamic_slice_in_dim(order_row, row_start, qblock, 0)
        grad_q = lax.dynamic_slice_in_dim(d_heads, row_start, qblock, 0)
        scores = masked_scores(rows_q, k_rot, seg_q, ord_q, segment, order_row, score_scale)
        probs = jnp.exp(scores - log_norms[block_idx][..., None])
        value_acc = value_acc + jnp.einsum(
            "hqk,qhd->khd", probs.astype(to_brainfloat), grad_q, preferred_element_type=f32
        )
        d_probs = jnp.einsum("qhd,khd->hqk", grad_q, v_all, preferred_element_type=f32)
        d_scores = (probs * (d_probs - jnp.sum(probs * d_probs, axis=-1, keepdims=True))).astype(
            to_brainfloat
        )
        query_grad = (
            jnp.einsum("hqk,khd->qhd", d_scores, k_rot, preferred_element_type=f32) * score_scale
        )
        key_acc = (
            key_acc
            + jnp.einsum("hqk,qhd->khd", d_scores, rows_q, preferred_element_type=f32) * score_scale
        )
        return ((key_acc, value_acc), query_grad)

    zero_heads = jnp.zeros(heads_shape, f32)
    (key_grad, value_grad), query_grads = lax.scan(
        attend_back, (zero_heads, zero_heads), jnp.arange(block_count, dtype=jnp.int32)
    )
    flat_width = head_count * HEAD_DIM
    grad_q_heads = (
        unrotate(query_grads.reshape(heads_shape), cosine, sine_tab)
        .reshape(group_rows, flat_width)
        .astype(to_brainfloat)
    )
    grad_k_heads = (
        unrotate(key_grad, cosine, sine_tab).reshape(group_rows, flat_width).astype(to_brainfloat)
    )
    grad_v_heads = value_grad.reshape(group_rows, flat_width).astype(to_brainfloat)
    tok_q, tok_k, tok_v = (
        lax.all_to_all(grad_q_heads, "seq", split_axis=0, concat_axis=1, tiled=True),
        lax.all_to_all(grad_k_heads, "seq", split_axis=0, concat_axis=1, tiled=True),
        lax.all_to_all(grad_v_heads, "seq", split_axis=0, concat_axis=1, tiled=True),
    )
    grads_tok = [tok_q, tok_k, tok_v]
    in_qkv = []
    out_qkv = []
    back_sum = jnp.zeros((rows_dev, MODEL_WIDTH), f32)
    for projection_index in range(3):
        input_factor_gradient, output_factor_gradient, input_gradient = low_rank_backward(
            normalized_brain,
            grads_tok[projection_index],
            query_key_value_inner[projection_index],
            first_factors_width[projection_index],
            second_factors_width[projection_index],
            select_adapter,
        )
        in_qkv.append(input_factor_gradient)
        out_qkv.append(output_factor_gradient)
        back_sum = back_sum + input_gradient
    grad_qkv = jnp.concatenate(grads_tok, axis=1)
    d_normed = col_product(
        grad_qkv, lax.all_gather(query_key_value_weight, "wshard", axis=0, tiled=True)
    )
    d_normed = d_normed + back_sum
    grad_tokens = (d_hidden_in + norm_backward(d_normed, scaled_one, inverse_one, gain_one)).astype(
        to_brainfloat
    )
    stacked_in_d = jnp.stack(
        [in_qkv[0], in_qkv[1], in_qkv[2], output_first_factor, gate_first_factor, up_first_factor]
    )
    stacked_out_d = jnp.stack(
        [out_qkv[0], out_qkv[1], out_qkv[2], output_second_factor, down_second_factor]
    )
    stacked_out_ff = jnp.stack([gate_second_factor, up_second_factor])
    sum_in_d, sum_in_ff, sum_out_d, sum_out_ff = (
        lax.psum_scatter(stacked_in_d, ("seq", "wshard"), scatter_dimension=2, tiled=True),
        lax.psum_scatter(down_first_factor, ("seq", "wshard"), scatter_dimension=1, tiled=True),
        lax.psum_scatter(stacked_out_d, ("seq", "wshard"), scatter_dimension=2, tiled=True),
        lax.psum_scatter(stacked_out_ff, ("seq", "wshard"), scatter_dimension=2, tiled=True),
    )
    return (mixed[None], grad_tokens[None], sum_in_d, sum_in_ff, sum_out_d, sum_out_ff)


def solution(mesh):
    in_specs = (
        P("wshard", "seq", None),
        P("wshard", "seq", None),
        P("wshard", None),
        P("wshard", None),
        P("wshard", None),
        P(),
        P(),
        P("wshard", None),
        P(),
        P("wshard", None),
        P(),
        P(),
        P("wshard", None),
        P("wshard", None),
        P(),
        P(),
        P(),
        P(),
    )
    out_specs = (
        P("wshard", "seq", None),
        P("wshard", "seq", None),
        P(None, None, ("seq", "wshard")),
        P(None, ("seq", "wshard")),
        P(None, None, ("seq", "wshard")),
        P(None, None, ("seq", "wshard")),
    )
    return jax.shard_map(local, mesh=mesh, in_specs=in_specs, out_specs=out_specs, check_vma=False)
```

profile of v0, /device:TPU:0, one launch (start us, length us, event | category | flops | bytes accessed | tf_op | source)
XLA Modules:
  0.0 3261.8 jit_solution(14730661479742907789)
XLA Ops:
  22.5 470.1 %all-gather.5.cloned.1.call-done = bf16[2048,6144]{1,0:T(8,128)(2,1)} async-done(((bf16[256,6144]{1,0:T(8,128)(2,1)}), bf16[2048,6144]{1,0:T(8,128)(2,1)}) %all-gather.5.cloned.1.call-update) | async-done | bytes 25165840 | tf_op jit(solution)/shard_map/all_gather | solution.py:182
  492.7 20.9 convolution_add_fusion.1
  529.0 18.4 all-to-all-done
  559.1 18.6 all-to-all-done.1
  623.2 196.2 %while.27 = (s32[]{:T(128)}, bf16[4,512,8,64]{1,3,2,0:T(8,128)(2,1)}, f32[4,8,512]{2,1,0:T(8,128)}, s32[4]{0:T(128)S(1)}, s32[2048]{0:T(1024)S(1)}, /*index=5*/s...) while((s32[]{:T(128)}, ...), condition=%wide.region_9.10_spmd, body=%wide.region_6.9_spmd.sunk | while | flops 2251288576 | bytes 110784728 | solution.py:228
  625.7 15.3 fusion.266
  656.1 15.7 fusion.268
  674.9 15.2 fusion.266
  705.2 15.8 fusion.268
  724.0 15.1 fusion.266
  754.2 15.6 fusion.268
  788.0 15.1 fusion.267
  803.1 15.7 fusion.268
  824.5 110.8 %all-gather.11.cloned.1.call-done = bf16[5632,2048]{1,0:T(8,128)(2,1)} async-done(((bf16[704,2048]{1,0:T(8,128)(2,1)}), bf16[5632,2048]{1,0:T(8,128)(2,1)}) %all-gather.11.cloned.1.call-update) | async-done | bytes 23068688 | tf_op jit(solution)/shard_map/all_gather | solution.py:260
  935.3 19.0 fusion.75
  967.7 94.2 %all-gather.7.cloned.1.call-done = bf16[2048,2048]{1,0:T(8,128)(2,1)} async-done(((bf16[256,2048]{1,0:T(8,128)(2,1)}), bf16[2048,2048]{1,0:T(8,128)(2,1)}) %all-gather.7.cloned.1.call-update) | async-done | bytes 8388624 | tf_op jit(solution)/shard_map/all_gather | solution.py:233
  1078.8 856.3 %all-gather.9.cloned.1.call-done = bf16[2048,11264]{1,0:T(8,128)(2,1)} async-done(((bf16[256,11264]{1,0:T(8,128)(2,1)}), bf16[2048,11264]{1,0:T(8,128)(2,1)}) %all-gather.9.cloned.1.call-update) | async-done | bytes 46137360 | tf_op jit(solution)/shard_map/all_gather | solution.py:243
  1935.1 31.9 fusion.176
  1977.3 18.6 multiply_convert_fusion.2
  2008.3 32.0 fusion.24
  2068.6 19.7 all-to-all-done.4
  2099.2 547.6 %while.28 = (s32[]{:T(128)}, f32[2048,8,64]{0,2,1:T(8,128)}, f32[2048,8,64]{0,2,1:T(8,128)}, f32[4,512,8,64]{1,0,3,2:T(4,128)}, s32[4]{0:T(128)}, /*index=5*/bf1...) while((s32[]{:T(128)}, f32[2048,8,64]{0,2,1:T(8,128)}, ...), condition=%wide.region_16.17_spmd.clone, body=%wide.region_14.16_spmd.clone.sunk | while | flops 5452853248 | bytes 284274944 | solution.py:350
  2101.4 17.4 fusion.278
  2122.7 25.4 multiply_reduce_fusion.4
  2148.1 27.4 multiply_convert_fusion.5
  2186.5 15.9 bitcast_add_fusion.5
  2213.2 21.1 dynamic_update_slice.19
  2236.4 17.4 fusion.278
  2257.6 25.4 multiply_reduce_fusion.4
  2283.0 27.4 multiply_convert_fusion.5
  2322.6 17.1 bitcast_add_fusion.5
  2350.6 21.1 dynamic_update_slice.19
  2373.7 17.4 fusion.278
  2394.9 25.4 multiply_reduce_fusion.4
  2420.3 27.4 multiply_convert_fusion.5
  2459.9 17.1 bitcast_add_fusion.5
  2487.9 21.1 dynamic_update_slice.19
  2511.0 17.4 fusion.278
  2532.3 25.4 multiply_reduce_fusion.4
  2557.6 27.4 multiply_convert_fusion.5
  2597.2 17.2 bitcast_add_fusion.5
  2625.3 21.1 dynamic_update_slice.19
  2716.9 22.8 all-to-all-done.5
  2754.8 20.9 all-to-all-done.7
  2822.8 17.3 fusion.177
  2851.0 22.3 fusion.29
  2885.8 180.6 %reduce-scatter.5.cloned.1.call-done = f32[5,2048,4]{1,0,2:T(8,128)} async-done(((f32[5,2048,128]{1,0,2:T(8,128)}), f32[5,2048,4]{1,0,2:T(8,128)}) %reduce-scatter.5.cloned.1.call-update) | async-done | bytes 163856 | tf_op jit(solution)/shard_map/reduce_scatter | solution.py:402
  3068.2 184.8 %reduce-scatter.3.cloned.1.call-done = f32[6,2048,4]{1,0,2:T(8,128)} async-done(((f32[6,2048,128]{1,0,2:T(8,128)}), f32[6,2048,4]{1,0,2:T(8,128)}) %reduce-scatter.3.cloned.1.call-update) | async-done | bytes 196624 | tf_op jit(solution)/shard_map/reduce_scatter | solution.py:400
  (366 shorter events, 516.3 us)
Async XLA Ops:
  7.2 947.1 %copy-start = (bf16[5632,128]{1,0:T(8,128)(2,1)S(1)}, bf16[5632,128]{1,0:T(8,128)(2,1)}, u32[]{:S(2)}) copy-start(bf16[5632,128]{1,0:T(8,128)(2,1)} %param.37) | copy-start | bytes 4325380
  7.2 485.5 %all-gather.5.cloned.1.call-start = ((), (), s32[]{:S(2)}) async-start(), calls=%async_computation.10 | async-start | bytes 28311552 | tf_op jit(solution)/shard_map/all_gather | solution.py:182
  7.9 927.3 %all-gather.11.cloned.1.call-start = ((), (), s32[]{:S(2)}) async-start(), calls=%async_computation.13 | async-start | bytes 25952256 | tf_op jit(solution)/shard_map/all_gather | solution.py:260
  8.7 8.1 copy-start.5
  8.7 1053.2 %all-gather.7.cloned.1.call-start = ((), (), s32[]{:S(2)}) async-start(), calls=%async_computation.11 | async-start | bytes 9437184 | tf_op jit(solution)/shard_map/all_gather | solution.py:233
  9.4 1925.6 %all-gather.9.cloned.1.call-start = ((), (), s32[]{:S(2)}) async-start(), calls=%async_computation.12 | async-start | bytes 51904512 | tf_op jit(solution)/shard_map/all_gather | solution.py:243
  492.7 20.9 copy-start.41
  518.2 29.2 all-to-all-start
  547.5 10.1 copy-start.22
  547.5 30.2 all-to-all-start.1
  557.6 28.1 copy-start.15
  577.6 32.3 all-to-all-start.2
  819.5 134.8 %copy-start.29 = (s32[2048]{0:T(1024)}, s32[2048]{0:T(1024)S(1)}, u32[]{:S(2)}) copy-start(s32[2048]{0:T(1024)S(1)} %get-tuple-element.603) | copy-start | bytes 24580
  819.5 115.8 %copy-start.16 = (bf16[1,512,2048]{2,1,0:T(8,128)(2,1)S(1)}, bf16[1,512,2048]{2,1,0:T(8,128)(2,1)}, u32[]{:S(2)}) copy-start(bf16[1,512,2048]{2,1,0:T(8,128)(2,1)} %param.23) | copy-start | bytes 6291460
  819.5 145.1 %all-to-all-start.3 = ((bf16[4,512,512]{1,2,0:T(8,128)(2,1)}), bf16[4,512,512]{1,2,0:T(8,128)(2,1)}, u32[]{:S(2)}, u32[]{:S(2)}) async-start(bf16[4,512,512]{1,2,0:T(8,128)(2,1)} %bitcast.386), calls=%async_computation.3 | async-start | bytes 4194304 | tf_op jit(solution)/shard_map/all_to_all | solution.py:230
  954.3 10.2 copy-start.70
  954.3 10.2 copy-start.76
  967.6 102.0 %copy-start.6 = (bf16[1,512,2048]{2,1,0:T(8,128)(2,1)S(1)}, bf16[1,512,2048]{2,1,0:T(8,128)(2,1)}, u32[]{:S(2)}) copy-start(bf16[1,512,2048]{2,1,0:T(8,128)(2,1)} %param.22) | copy-start | bytes 6291460
  1061.9 7.8 copy-start.46
  1073.6 893.4 %copy-start.10 = (bf16[512,2048]{1,0:T(8,128)(2,1)}, bf16[512,2048]{1,0:T(8,128)(2,1)S(1)}, u32[]{:S(2)}) copy-start(bf16[512,2048]{1,0:T(8,128)(2,1)S(1)} %add_convert_fusion.2) | copy-start | bytes 6291460
  1935.1 31.9 copy-start.33
  1935.1 31.9 copy-start.36
  2000.7 39.5 %copy-start.37 = (bf16[512,128]{1,0:T(8,128)(2,1)}, bf16[512,128]{1,0:T(8,128)(2,1)S(1)}, u32[]{:S(2)}) copy-start(bf16[512,128]{1,0:T(8,128)(2,1)S(1)} %fusion.110) | copy-start | bytes 393220
  2008.2 32.0 copy-start.55
  2008.2 32.0 copy-start.59
  2008.3 32.0 copy-start.63
  2040.3 10.8 slice-start.2
  2059.0 29.2 all-to-all-start.4
  2089.5 9.7 copy-start.1
  2089.5 9.7 copy-start.28
  2089.5 9.7 copy-start.30
  2665.3 38.4 %all-to-all-start.6 = ((bf16[4,512,512]{1,2,0:T(8,128)(2,1)}), bf16[4,512,512]{1,2,0:T(8,128)(2,1)S(1)}, u32[]{:S(2)}, u32[]{:S(2)}) async-start(bf16[4,512,512]{1,2,0:T(8,128)(2,1)} %copy.103), calls=%async_computation.6 | async-start | bytes 4194304 | tf_op jit(solution)/shard_map/all_to_all | solution.py:365
  2668.9 213.7 %all-reduce.5.cloned.1.call-start = ((), (), s32[]{:S(2)}) async-start(), calls=%async_computation.16 | async-start | bytes 17301504
  2703.7 36.0 %all-to-all-start.5 = ((bf16[4,512,512]{1,2,0:T(8,128)(2,1)}), bf16[4,512,512]{1,2,0:T(8,128)(2,1)}, u32[]{:S(2)}, u32[]{:S(2)}) async-start(bf16[4,512,512]{1,2,0:T(8,128)(2,1)} %copy.102), calls=%async_computation.5 | async-start | bytes 4194304 | tf_op jit(solution)/shard_map/all_to_all | solution.py:364
  2713.5 30.7 copy-start.71
  2713.5 30.8 copy-start.77
  2739.7 36.0 %all-to-all-start.7 = ((bf16[4,512,512]{1,2,0:T(8,128)(2,1)}), bf16[4,512,512]{1,2,0:T(8,128)(2,1)}, u32[]{:S(2)}, u32[]{:S(2)}) async-start(bf16[4,512,512]{1,2,0:T(8,128)(2,1)} %copy.104), calls=%async_computation.7 | async-start | bytes 4194304 | tf_op jit(solution)/shard_map/all_to_all | solution.py:366
  2744.2 8.9 copy-start.20
  2744.2 322.2 %reduce-scatter.5.cloned.1.call-start = ((), (), s32[]{:S(2)}) async-start(), calls=%async_computation.15 | async-start | bytes 8650752 | tf_op jit(solution)/shard_map/reduce_scatter | solution.py:402
  2744.3 8.8 copy-start.44
  2793.1 7.6 copy-start.7
  2793.1 7.6 copy-start.57
  2793.2 7.6 copy-start.61
  2793.2 7.6 copy-start.68
  2793.2 459.8 %reduce-scatter.3.cloned.1.call-start = ((), (), s32[]{:S(2)}) async-start(), calls=%async_computation.14 | async-start | bytes 8650752 | tf_op jit(solution)/shard_map/reduce_scatter | solution.py:400
  2796.2 8.8 copy-start.49
  2822.8 17.4 copy-start.4
  2822.8 17.4 copy-start.40
  (50 other events, 202.7 us)
Sparse Core Ops, SparseCore 0:
  9.5 483.0 all-gather.4
  494.2 441.0 all-gather.10
  937.4 124.4 all-gather.6
  1063.3 871.7 all-gather.8
  2691.3 188.5 all-reduce.4
  2882.1 184.3 reduce-scatter.4
  3068.7 184.2 reduce-scatter.2
where the time goes:
time: 3280 us; the launch traced here: 3260 us
  waiting for transfers between devices  2000 us (61%)
  matrix products  764 us (23%)
  other arithmetic  219 us (7%)
  local copies, waits for them, and re-layouts  215 us (7%)
  starting transfers between devices  34.3 us (1%)
    all_gather x1, waiting for transfers between devices, local(): lax.all_gather(gate_up_weight, 'wshard', axis=0, tiled=True)  856 us
    all_gather x1, waiting for transfers between devices, local(): lax.all_gather(query_key_value_weight, 'wshard', axis=0, tiled=True)  470 us
    reduce_scatter x1, waiting for transfers between devices, local(): lax.psum_scatter(stacked_in_d, ('seq', 'wshard'), scatter_dimension=2, ti...  185 us
    reduce_scatter x1, waiting for transfers between devices, local(): lax.psum_scatter(stacked_out_d, ('seq', 'wshard'), scatter_dimension=2, t...  181 us
    dot_general x8, matrix products, masked_scores(): jnp.einsum('qhd,khd->hqk', rows_q, k_rot, preferred_element_type=jnp.floa...  162 us
    all_gather x1, waiting for transfers between devices, local(): lax.all_gather(down_weight, 'wshard', axis=0, tiled=True)  111 us
    convert_element_type x4, other arithmetic, attend_back(): (probs * (d_probs - jnp.sum(probs * d_probs, axis=-1, keepdims=True))).as...  110 us
    all_gather x1, waiting for transfers between devices, local(): lax.all_gather(attention_output_weight, 'wshard', axis=0, tiled=True)  94.2 us
  transfers between devices with their start and end apart: 15, of which 11 were waited for; matrix products, arithmetic and copies ran while one was open for 15% of the time, Pallas kernels for 0%

commit v1 on v0

--- a/solution.py
+++ b/solution.py
@@ -121,6 +121,13 @@
         reverse_result, low_rank_first, CONTRACT_FINAL, preferred_element_type=jnp.float32
     )
     return (input_factor_gradient, output_factor_gradient, input_gradient)
+
+
+def gather_rows(shard):
+    parts = lax.axis_size("seq")
+    rows = shard.shape[0] // parts
+    own = lax.dynamic_slice_in_dim(shard, lax.axis_index("seq") * rows, rows, 0)
+    return lax.all_gather(own, ("wshard", "seq"), axis=0, tiled=True)
 
 
 def row_fold(product_operand, weight_rows):
@@ -179,7 +186,7 @@
     )
     normalized_brain = normed.astype(to_brainfloat)
     joint_qkv = row_fold(
-        normalized_brain, lax.all_gather(query_key_value_weight, "wshard", axis=0, tiled=True)
+        normalized_brain, gather_rows(query_key_value_weight)
     )
     joint_qkv = joint_qkv + query_key_value_bias.astype(f32)
     query_key_value_inner = [
@@ -230,7 +237,7 @@
     attention_tokens = lax.all_to_all(attended, "seq", split_axis=0, concat_axis=1, tiled=True)
     output_inner_rows = low_rank_inner(attention_tokens, first_factors_width[3], select_adapter)
     residual_branch = row_fold(
-        attention_tokens, lax.all_gather(attention_output_weight, "wshard", axis=0, tiled=True)
+        attention_tokens, gather_rows(attention_output_weight)
     )
     incoming_hidden = (
         input_rows + residual_branch + apply_low_rank(output_inner_rows, second_factors_width[3])
@@ -240,7 +247,7 @@
     )
     normalized_second_brain = normed_two.astype(to_brainfloat)
     joint_gate_up = row_fold(
-        normalized_second_brain, lax.all_gather(gate_up_weight, "wshard", axis=0, tiled=True)
+        normalized_second_brain, gather_rows(gate_up_weight)
     )
     gate_inner_rows = low_rank_inner(
         normalized_second_brain, first_factors_width[4], select_adapter
@@ -257,7 +264,7 @@
     hidden_state = (silu_gate * up_activation).astype(to_brainfloat)
     down_inner_rows = low_rank_inner(hidden_state, first_factors_hidden, select_adapter)
     residual_branch_second = row_fold(
-        hidden_state, lax.all_gather(down_weight, "wshard", axis=0, tiled=True)
+        hidden_state, gather_rows(down_weight)
     )
     mixed = (
         incoming_hidden
@@ -275,7 +282,7 @@
         select_adapter,
     )
     d_hidden = col_product(
-        mixed_gradient, lax.all_gather(down_weight, "wshard", axis=0, tiled=True)
+        mixed_gradient, gather_rows(down_weight)
     )
     d_hidden = d_hidden + down_reverse
     gate_gradient = (
@@ -300,7 +307,7 @@
     )
     grad_gu = jnp.concatenate([gate_gradient, up_gradient], axis=1)
     d_normed_two = col_product(
-        grad_gu, lax.all_gather(gate_up_weight, "wshard", axis=0, tiled=True)
+        grad_gu, gather_rows(gate_up_weight)
     )
     d_normed_two = d_normed_two + gate_reverse + up_reverse
     d_hidden_in = grad_top + norm_backward(d_normed_two, scaled_two, inverse_two, gain_two)
@@ -314,7 +321,7 @@
         select_adapter,
     )
     d_att = col_product(
-        branch_gradient, lax.all_gather(attention_output_weight, "wshard", axis=0, tiled=True)
+        branch_gradient, gather_rows(attention_output_weight)
     )
     d_att = (d_att + output_reverse).astype(to_brainfloat)
     d_heads = lax.all_to_all(d_att, "seq", split_axis=1, concat_axis=0, tiled=True).reshape(
@@ -383,7 +390,7 @@
         back_sum = back_sum + input_gradient
     grad_qkv = jnp.concatenate(grads_tok, axis=1)
     d_normed = col_product(
-        grad_qkv, lax.all_gather(query_key_value_weight, "wshard", axis=0, tiled=True)
+        grad_qkv, gather_rows(query_key_value_weight)
     )
     d_normed = d_normed + back_sum
     grad_tokens = (d_hidden_in + norm_backward(d_normed, scaled_one, inverse_one, gain_one)).astype(

time: 3280 us -> 2030 us (0.62)
  waiting for transfers between devices: 2000 us -> 781 us
    all_gather x4, waiting for transfers between devices: 1530 us -> 243 us  [gather_rows(): return lax.all_gather(own, ('wshard', 'seq'), axis=0, tiled=True)]
  transfers between devices with their start and end apart: 15 -> 15, of which waited for: 11 -> 11; matrix products, arithmetic and copies ran while one was open for 15% -> 24% of each run, Pallas kernels for 0% -> 0%
where the time goes in v1:
time: 2030 us; the launch traced here: 2020 us
  waiting for transfers between devices  781 us (38%)
  matrix products  754 us (37%)
  local copies, waits for them, and re-layouts  214 us (11%)
  other arithmetic  206 us (10%)
  starting transfers between devices  34.3 us (2%)
    all_gather x4, waiting for transfers between devices, gather_rows(): return lax.all_gather(own, ('wshard', 'seq'), axis=0, tiled=True)  243 us
    reduce_scatter x1, waiting for transfers between devices, local(): lax.psum_scatter(stacked_in_d, ('seq', 'wshard'), scatter_dimension=2, ti...  185 us
    reduce_scatter x1, waiting for transfers between devices, local(): lax.psum_scatter(stacked_out_d, ('seq', 'wshard'), scatter_dimension=2, t...  182 us
    dot_general x8, matrix products, masked_scores(): jnp.einsum('qhd,khd->hqk', rows_q, k_rot, preferred_element_type=jnp.floa...  161 us
    convert_element_type x4, other arithmetic, attend_back(): (probs * (d_probs - jnp.sum(probs * d_probs, axis=-1, keepdims=True))).as...  110 us
    dynamic_update_slice x8, local copies, waits for them, and re-layouts, local(): lax.map(attend, jnp.arange(block_count, dtype=jnp.int32))  88.5 us
    dot_general x4, matrix products, row_fold(): jnp.dot(product_operand, weight_rows, preferred_element_type=jnp.float32)  77.6 us
    dot_general x4, matrix products, col_product(): lax.dot_general(row_gradients, weight_rows, CONTRACT_FINAL, preferred_ele...  76.1 us
  transfers between devices with their start and end apart: 15, of which 11 were waited for; matrix products, arithmetic and copies ran while one was open for 24% of the time, Pallas kernels for 0%

profile of v1, /device:TPU:0, one launch (start us, length us, event | category | flops | bytes accessed | tf_op | source)
XLA Modules:
  0.0 2018.6 jit_solution(17993388597933860906)
XLA Ops:
  22.3 145.9 %all-gather.5.cloned.1.call-done = bf16[2048,6144]{1,0:T(8,128)(2,1)} async-done(((bf16[64,6144]{1,0:T(8,128)(2,1)}), bf16[2048,6144]{1,0:T(8,128)(2,1)}) %all-gather.5.cloned.1.call-update) | async-done | bytes 25165840 | tf_op jit(solution)/shard_map/all_gather | solution.py:130
  168.2 20.9 %convolution_add_fusion = f32[512,6144]{1,0:T(8,128)} fusion(bf16[2048,6144]{1,0:T(8,128)(2,1)} %all-gather.5.cloned.1.call-done, f32[6144]{0:T(1024)S(1)} %convert_element_type.184, bf16[1,512,2048]{2,1,0:T(8,128)(2,1)S(1)} %copy-done.7, f32[2048]{0:T(1024)S(1)} %convert_element_type.182, f32[2048]{0:T(1024)S(1)} %convert_element_type.181, ...), kind=kOutput, calls=%fused_computation.47 | convolution fusion | flops 12894339072 | bytes 39890944 | tf_op jit(solution)/shard_map/dot_general | solution.py:134
  204.5 37.6 %all-to-all-done = bf16[512,4,512]{2,0,1:T(8,128)(2,1)S(1)} async-done(((bf16[512,4,512]{2,0,1:T(8,128)(2,1)}), bf16[512,4,512]{2,0,1:T(8,128)(2,1)S(1)}, u32[]{:S(2)}, u32[]{:S(2)}) %all-to-all-start) | async-done | bytes 2097184 | tf_op jit(solution)/shard_map/all_to_all | solution.py:206
  253.6 29.4 %all-to-all-done.1 = bf16[512,4,512]{2,0,1:T(8,128)(2,1)} async-done(((bf16[512,4,512]{2,0,1:T(8,128)(2,1)}), bf16[512,4,512]{2,0,1:T(8,128)(2,1)}, u32[]{:S(2)}, u32[]{:S(2)}) %all-to-all-start.1) | async-done | bytes 2097184 | tf_op jit(solution)/shard_map/all_to_all | solution.py:207
  312.9 23.2 %all-to-all-done.2 = bf16[512,4,512]{2,0,1:T(8,128)(2,1)} async-done(((bf16[512,4,512]{2,0,1:T(8,128)(2,1)}), bf16[512,4,512]{2,0,1:T(8,128)(2,1)}, u32[]{:S(2)}, u32[]{:S(2)}) %all-to-all-start.2) | async-done | bytes 2097184 | tf_op jit(solution)/shard_map/all_to_all | solution.py:208
  346.5 196.2 %while.27 = (s32[]{:T(128)}, bf16[4,512,8,64]{1,3,2,0:T(8,128)(2,1)}, f32[4,8,512]{2,1,0:T(8,128)}, s32[4]{0:T(128)S(1)}, s32[2048]{0:T(1024)S(1)}, /*index=5*/s...) while((s32[]{:T(128)}, ...), condition=%wide.region_9.10_spmd, body=%wide.region_6.9_spmd.sunk | while | flops 2251288576 | bytes 110784728 | solution.py:235
  348.8 15.4 fusion.266
  364.2 15.1 fusion.267
  379.3 15.8 fusion.268
  398.0 15.8 fusion.266
  413.8 15.1 fusion.267
  428.9 16.0 fusion.268
  462.8 15.1 fusion.267
  477.8 15.6 fusion.268
  526.2 15.9 fusion.268
  547.6 17.2 fusion.75
  601.7 97.4 %all-gather.9.cloned.1.call-done = bf16[2048,11264]{1,0:T(8,128)(2,1)} async-done(((bf16[64,11264]{1,0:T(8,128)(2,1)}), bf16[2048,11264]{1,0:T(8,128)(2,1)}) %all-gather.9.cloned.1.call-update) | async-done | bytes 46137360 | tf_op jit(solution)/shard_map/all_gather | solution.py:130
  699.0 31.7 %fusion.176 = f32[512,11264]{1,0:T(8,128)} fusion(bf16[512,2048]{1,0:T(8,128)(2,1)S(1)} %add_convert_fusion.2, bf16[2048,11264]{1,0:T(8,128)(2,1)} %all-gather.9.cloned.1.call-done), kind=kOutput, calls=%fused_computation.267 | convolution fusion | flops 23622320128 | bytes 71303168 | tf_op jit(solution)/shard_map/dot_general | solution.py:134
  740.9 20.0 multiply_convert_fusion.2
  771.5 32.1 %fusion.24 = f32[512,2048]{1,0:T(8,128)} fusion(bf16[2048,11264]{1,0:T(8,128)(2,1)} %all-gather.9.cloned.1.call-done, bf16[512,5632]{1,0:T(8,128)(2,1)} %get-tuple-element.293, bf16[512,5632]{1,0:T(8,128)(2,1)} %get-tuple-element.292), kind=kOutput, calls=%fused_computation.37 | convolution fusion | flops 23645388800 | bytes 61865984 | tf_op jit(solution)/shard_map/dot_general | solution.py:138
  831.7 19.7 all-to-all-done.4
  861.8 537.6 %while.28 = (s32[]{:T(128)}, f32[2048,8,64]{0,2,1:T(8,128)}, f32[2048,8,64]{0,2,1:T(8,128)}, f32[4,512,8,64]{1,0,3,2:T(4,128)}, s32[4]{0:T(128)S(1)}, /*index=5*...) while((s32[]{:T(128)}, f32[2048,8,64]{0,2,1:T(8,128)}, ...), condition=%wide.region_16.17_spmd.clone, body=%wide.region_14.16_spmd.clone.sunk | while | flops 5452853248 | bytes 284274944 | solution.py:357
  863.3 17.4 fusion.278
  884.4 24.9 %multiply_reduce_fusion.4 = (f32[8,512]{1,0:T(8,128)S(1)}, f32[8,512,2048]{2,1,0:T(8,128)}) fusion(f32[8,512,2048]{2,1,0:T(8,128)} %fusion.278, f32[8,512]{1,0:T(8,128)S(1)} %dynamic-slice_bitcast_fusion.2, bf16[2048,8,64]{0,2,1:T(8,128)(2,1)S(1)} %get-tuple-element.550, bf16[2048,8,64]{0,2,1:T(8,128)(2,1)} %get-tuple-element.546, ...), kind=kOutput, calls=%fused_computation.16.clone.1 | convolution fusion | flops 1115680768 | bytes 70811648 | tf_op jit(solution)/shard_map/while/body/eval_jaxpr/qhd,khd->hqk/dot_general | solution.py:145
  909.2 27.4 %multiply_convert_fusion.5 = bf16[8,512,2048]{2,1,0:T(8,128)(2,1)} fusion(f32[8,512,2048]{2,1,0:T(8,128)} %get-tuple-element.461, f32[8,512,2048]{2,1,0:T(8,128)} %fusion.278, f32[8,512]{1,0:T(8,128)S(1)} %get-tuple-element.462), kind=kLoop, calls=%fused_computation.15.clone.1 | loop fusion | flops 25165824 | bytes 83902464 | tf_op jit(solution)/shard_map/while/body/eval_jaxpr/convert_element_type | solution.py:344
  947.7 15.9 bitcast_add_fusion.6
  973.4 21.0 %dynamic_update_slice.19 = f32[4,512,8,64]{1,0,3,2:T(4,128)} dynamic-update-slice(f32[4,512,8,64]{1,0,3,2:T(4,128)} %get-tuple-element.526, f32[1,512,8,64]{1,0,3,2:T(1,128)S(1)} %copy.143, s32[]{:T(128)S(6)} %copy.160, s32[]{:T(128)} %constant.87.clone.1..sunk.1, s32[]{:T(128)} %constant.87.clone.1..sunk.1, s32[]{:T(128)} %constant.87.clone.1..sunk.1) | dynamic-update-slice | bytes 2097156 | tf_op jit(solution)/shard_map/while/body/jit(dynamic_update_index_in_dim)/dynamic_update_slice | solution.py:235
  995.7 17.4 fusion.278
  1016.8 24.9 %multiply_reduce_fusion.4 = (f32[8,512]{1,0:T(8,128)S(1)}, f32[8,512,2048]{2,1,0:T(8,128)}) fusion(f32[8,512,2048]{2,1,0:T(8,128)} %fusion.278, f32[8,512]{1,0:T(8,128)S(1)} %dynamic-slice_bitcast_fusion.2, bf16[2048,8,64]{0,2,1:T(8,128)(2,1)S(1)} %get-tuple-element.550, bf16[2048,8,64]{0,2,1:T(8,128)(2,1)} %get-tuple-element.546, ...), kind=kOutput, calls=%fused_computation.16.clone.1 | convolution fusion | flops 1115680768 | bytes 70811648 | tf_op jit(solution)/shard_map/while/body/eval_jaxpr/qhd,khd->hqk/dot_general | solution.py:145
  1041.7 27.4 %multiply_convert_fusion.5 = bf16[8,512,2048]{2,1,0:T(8,128)(2,1)} fusion(f32[8,512,2048]{2,1,0:T(8,128)} %get-tuple-element.461, f32[8,512,2048]{2,1,0:T(8,128)} %fusion.278, f32[8,512]{1,0:T(8,128)S(1)} %get-tuple-element.462), kind=kLoop, calls=%fused_computation.15.clone.1 | loop fusion | flops 25165824 | bytes 83902464 | tf_op jit(solution)/shard_map/while/body/eval_jaxpr/convert_element_type | solution.py:344
  1081.3 17.1 bitcast_add_fusion.6
  1108.3 21.0 %dynamic_update_slice.19 = f32[4,512,8,64]{1,0,3,2:T(4,128)} dynamic-update-slice(f32[4,512,8,64]{1,0,3,2:T(4,128)} %get-tuple-element.526, f32[1,512,8,64]{1,0,3,2:T(1,128)S(1)} %copy.143, s32[]{:T(128)S(6)} %copy.160, s32[]{:T(128)} %constant.87.clone.1..sunk.1, s32[]{:T(128)} %constant.87.clone.1..sunk.1, s32[]{:T(128)} %constant.87.clone.1..sunk.1) | dynamic-update-slice | bytes 2097156 | tf_op jit(solution)/shard_map/while/body/jit(dynamic_update_index_in_dim)/dynamic_update_slice | solution.py:235
  1130.6 17.4 fusion.278
  1151.7 24.9 %multiply_reduce_fusion.4 = (f32[8,512]{1,0:T(8,128)S(1)}, f32[8,512,2048]{2,1,0:T(8,128)}) fusion(f32[8,512,2048]{2,1,0:T(8,128)} %fusion.278, f32[8,512]{1,0:T(8,128)S(1)} %dynamic-slice_bitcast_fusion.2, bf16[2048,8,64]{0,2,1:T(8,128)(2,1)S(1)} %get-tuple-element.550, bf16[2048,8,64]{0,2,1:T(8,128)(2,1)} %get-tuple-element.546, ...), kind=kOutput, calls=%fused_computation.16.clone.1 | convolution fusion | flops 1115680768 | bytes 70811648 | tf_op jit(solution)/shard_map/while/body/eval_jaxpr/qhd,khd->hqk/dot_general | solution.py:145
  1176.5 27.4 %multiply_convert_fusion.5 = bf16[8,512,2048]{2,1,0:T(8,128)(2,1)} fusion(f32[8,512,2048]{2,1,0:T(8,128)} %get-tuple-element.461, f32[8,512,2048]{2,1,0:T(8,128)} %fusion.278, f32[8,512]{1,0:T(8,128)S(1)} %get-tuple-element.462), kind=kLoop, calls=%fused_computation.15.clone.1 | loop fusion | flops 25165824 | bytes 83902464 | tf_op jit(solution)/shard_map/while/body/eval_jaxpr/convert_element_type | solution.py:344
  1216.1 17.1 bitcast_add_fusion.6
  1243.1 21.0 %dynamic_update_slice.19 = f32[4,512,8,64]{1,0,3,2:T(4,128)} dynamic-update-slice(f32[4,512,8,64]{1,0,3,2:T(4,128)} %get-tuple-element.526, f32[1,512,8,64]{1,0,3,2:T(1,128)S(1)} %copy.143, s32[]{:T(128)S(6)} %copy.160, s32[]{:T(128)} %constant.87.clone.1..sunk.1, s32[]{:T(128)} %constant.87.clone.1..sunk.1, s32[]{:T(128)} %constant.87.clone.1..sunk.1) | dynamic-update-slice | bytes 2097156 | tf_op jit(solution)/shard_map/while/body/jit(dynamic_update_index_in_dim)/dynamic_update_slice | solution.py:235
  1265.4 17.4 fusion.278
  1286.5 24.9 %multiply_reduce_fusion.4 = (f32[8,512]{1,0:T(8,128)S(1)}, f32[8,512,2048]{2,1,0:T(8,128)}) fusion(f32[8,512,2048]{2,1,0:T(8,128)} %fusion.278, f32[8,512]{1,0:T(8,128)S(1)} %dynamic-slice_bitcast_fusion.2, bf16[2048,8,64]{0,2,1:T(8,128)(2,1)S(1)} %get-tuple-element.550, bf16[2048,8,64]{0,2,1:T(8,128)(2,1)} %get-tuple-element.546, ...), kind=kOutput, calls=%fused_computation.16.clone.1 | convolution fusion | flops 1115680768 | bytes 70811648 | tf_op jit(solution)/shard_map/while/body/eval_jaxpr/qhd,khd->hqk/dot_general | solution.py:145
  1311.3 27.4 %multiply_convert_fusion.5 = bf16[8,512,2048]{2,1,0:T(8,128)(2,1)} fusion(f32[8,512,2048]{2,1,0:T(8,128)} %get-tuple-element.461, f32[8,512,2048]{2,1,0:T(8,128)} %fusion.278, f32[8,512]{1,0:T(8,128)S(1)} %get-tuple-element.462), kind=kLoop, calls=%fused_computation.15.clone.1 | loop fusion | flops 25165824 | bytes 83902464 | tf_op jit(solution)/shard_map/while/body/eval_jaxpr/convert_element_type | solution.py:344
  1351.0 17.2 bitcast_add_fusion.6
  1378.0 21.0 %dynamic_update_slice.19 = f32[4,512,8,64]{1,0,3,2:T(4,128)} dynamic-update-slice(f32[4,512,8,64]{1,0,3,2:T(4,128)} %get-tuple-element.526, f32[1,512,8,64]{1,0,3,2:T(1,128)S(1)} %copy.143, s32[]{:T(128)S(6)} %copy.160, s32[]{:T(128)} %constant.87.clone.1..sunk.1, s32[]{:T(128)} %constant.87.clone.1..sunk.1, s32[]{:T(128)} %constant.87.clone.1..sunk.1) | dynamic-update-slice | bytes 2097156 | tf_op jit(solution)/shard_map/while/body/jit(dynamic_update_index_in_dim)/dynamic_update_slice | solution.py:235
  1465.4 30.0 %all-to-all-done.5 = bf16[4,512,512]{1,2,0:T(8,128)(2,1)} async-done(((bf16[4,512,512]{1,2,0:T(8,128)(2,1)}), bf16[4,512,512]{1,2,0:T(8,128)(2,1)}, u32[]{:S(2)}, u32[]{:S(2)}) %all-to-all-start.5) | async-done | bytes 2097184 | tf_op jit(solution)/shard_map/all_to_all | solution.py:371
  1510.6 19.8 all-to-all-done.7
  1578.8 17.1 fusion.177
  1606.5 22.2 %fusion.29 = f32[512,2048]{1,0:T(8,128)} fusion(bf16[2048,6144]{1,0:T(8,128)(2,1)} %all-gather.5.cloned.1.call-done, bf16[512,2048]{0,1:T(8,128)(2,1)} %bitcast.377, bf16[512,2048]{0,1:T(8,128)(2,1)} %bitcast.40, bf16[512,2048]{0,1:T(8,128)(2,1)} %bitcast.38), kind=kOutput, calls=%fused_computation.50 | convolution fusion | flops 12903776256 | bytes 35651584 | tf_op jit(solution)/shard_map/dot_general | solution.py:138
  1641.1 182.2 %reduce-scatter.5.cloned.1.call-done = f32[5,2048,4]{1,0,2:T(8,128)} async-done(((f32[5,2048,128]{1,0,2:T(8,128)}), f32[5,2048,4]{1,0,2:T(8,128)}) %reduce-scatter.5.cloned.1.call-update) | async-done | bytes 163856 | tf_op jit(solution)/shard_map/reduce_scatter | solution.py:409
  1825.0 184.7 %reduce-scatter.3.cloned.1.call-done = f32[6,2048,4]{1,0,2:T(8,128)} async-done(((f32[6,2048,128]{1,0,2:T(8,128)}), f32[6,2048,4]{1,0,2:T(8,128)}) %reduce-scatter.3.cloned.1.call-update) | async-done | bytes 196624 | tf_op jit(solution)/shard_map/reduce_scatter | solution.py:407
  (378 shorter events, 488.4 us)
Async XLA Ops:
  7.2 161.0 %all-gather.5.cloned.1.call-start = ((), (), s32[]{:S(2)}) async-start(), calls=%async_computation.10 | async-start | bytes 25952256 | tf_op jit(solution)/shard_map/all_gather | solution.py:130
  10.1 537.6 %all-gather.11.cloned.1.call-start = ((), (), s32[]{:S(2)}) async-start(), calls=%async_computation.13 | async-start | bytes 23789568 | tf_op jit(solution)/shard_map/all_gather | solution.py:130
  12.3 573.6 %all-gather.7.cloned.1.call-start = ((), (), s32[]{:S(2)}) async-start(), calls=%async_computation.11 | async-start | bytes 8650752 | tf_op jit(solution)/shard_map/all_gather | solution.py:130
  14.1 685.0 %all-gather.9.cloned.1.call-start = ((), (), s32[]{:S(2)}) async-start(), calls=%async_computation.12 | async-start | bytes 47579136 | tf_op jit(solution)/shard_map/all_gather | solution.py:130
  16.9 151.3 %copy-start.65 = (f32[2048]{0:T(1024)}, f32[2048]{0:T(1024)S(1)}, u32[]{:S(2)}) copy-start(f32[2048]{0:T(1024)S(1)} %convert_element_type.182) | copy-start | bytes 24580
  17.0 151.3 %copy-start.57 = (f32[2048]{0:T(1024)}, f32[2048]{0:T(1024)S(1)}, u32[]{:S(2)}) copy-start(f32[2048]{0:T(1024)S(1)} %convert_element_type.181) | copy-start | bytes 24580
  17.3 271.6 %copy-start.71 = (s32[512]{0:T(512)}, s32[512]{0:T(512)S(1)}, u32[]{:S(2)}) copy-start(s32[512]{0:T(512)S(1)} %dynamic-slice.2) | copy-start | bytes 6148
  17.3 271.6 %copy-start.78 = (s32[128]{0:T(128)}, s32[128]{0:T(128)S(1)}, u32[]{:S(2)}) copy-start(s32[128]{0:T(128)S(1)} %and_select_fusion) | copy-start | bytes 1540
  17.7 150.5 %copy-start.61 = (f32[512]{0:T(512)}, f32[512]{0:T(512)S(1)}, u32[]{:S(2)}) copy-start(f32[512]{0:T(512)S(1)} %broadcast_multiply_fusion.5) | copy-start | bytes 6148
  18.4 170.7 %copy-start.68 = (f32[512]{0:T(512)}, f32[512]{0:T(512)S(1)}, u32[]{:S(2)}) copy-start(f32[512]{0:T(512)S(1)} %add_rsqrt_fusion.1) | copy-start | bytes 6148
  22.3 166.8 %copy-start.43 = (bf16[512,128]{1,0:T(8,128)(2,1)}, bf16[512,128]{1,0:T(8,128)(2,1)S(1)}, u32[]{:S(2)}) copy-start(bf16[512,128]{1,0:T(8,128)(2,1)S(1)} %fusion.94) | copy-start | bytes 393220
  193.7 48.4 %all-to-all-start = ((bf16[512,4,512]{2,0,1:T(8,128)(2,1)}), bf16[512,4,512]{2,0,1:T(8,128)(2,1)S(1)}, u32[]{:S(2)}, u32[]{:S(2)}) async-start(bf16[512,4,512]{2,0,1:T(8,128)(2,1)} %bitcast.383), calls=%async_computation | async-start | bytes 4194304 | tf_op jit(solution)/shard_map/all_to_all | solution.py:206
  242.1 10.0 copy-start.22
  242.1 40.9 %all-to-all-start.1 = ((bf16[512,4,512]{2,0,1:T(8,128)(2,1)}), bf16[512,4,512]{2,0,1:T(8,128)(2,1)}, u32[]{:S(2)}, u32[]{:S(2)}) async-start(bf16[512,4,512]{2,0,1:T(8,128)(2,1)} %bitcast.380), calls=%async_computation.1 | async-start | bytes 4194304 | tf_op jit(solution)/shard_map/all_to_all | solution.py:207
  252.1 35.6 %copy-start.76 = (bf16[2048]{0:T(1024)(128)(2,1)S(1)}, bf16[2048]{0:T(1024)(128)(2,1)}, u32[]{:S(2)}) copy-start(bf16[2048]{0:T(1024)(128)(2,1)} %param.33) | copy-start | bytes 12292
  252.1 36.2 %copy-start.77 = (bf16[2048]{0:T(1024)(128)(2,1)S(1)}, bf16[2048]{0:T(1024)(128)(2,1)}, u32[]{:S(2)}) copy-start(bf16[2048]{0:T(1024)(128)(2,1)} %param.32) | copy-start | bytes 12292
  252.1 36.8 %copy-start.18 = (bf16[1,512,2048]{2,1,0:T(8,128)(2,1)S(1)}, bf16[1,512,2048]{2,1,0:T(8,128)(2,1)}, u32[]{:S(2)}) copy-start(bf16[1,512,2048]{2,1,0:T(8,128)(2,1)} %param.23) | copy-start | bytes 6291460
  283.0 53.0 %all-to-all-start.2 = ((bf16[512,4,512]{2,0,1:T(8,128)(2,1)}), bf16[512,4,512]{2,0,1:T(8,128)(2,1)}, u32[]{:S(2)}, u32[]{:S(2)}) async-start(bf16[512,4,512]{2,0,1:T(8,128)(2,1)} %bitcast.379), calls=%async_computation.2 | async-start | bytes 4194304 | tf_op jit(solution)/shard_map/all_to_all | solution.py:208
  291.7 50.5 %copy-start.35 = (f32[2048,8]{0,1:T(8,128)}, f32[2048,8]{0,1:T(8,128)S(1)}, u32[]{:S(2)}) copy-start(f32[2048,8]{0,1:T(8,128)S(1)} %get-tuple-element.307) | copy-start | bytes 196612
  291.7 50.5 %copy-start.37 = (f32[2048,8]{0,1:T(8,128)}, f32[2048,8]{0,1:T(8,128)S(1)}, u32[]{:S(2)}) copy-start(f32[2048,8]{0,1:T(8,128)S(1)} %get-tuple-element.308) | copy-start | bytes 196612
  542.7 22.2 %copy-start.2 = (bf16[2048,8,64]{0,2,1:T(8,128)(2,1)}, bf16[2048,8,64]{0,2,1:T(8,128)(2,1)S(1)}, u32[]{:S(2)}) copy-start(bf16[2048,8,64]{0,2,1:T(8,128)(2,1)S(1)} %get-tuple-element.569) | copy-start | bytes 6291460
  542.7 22.2 %copy-start.29 = (s32[2048]{0:T(1024)}, s32[2048]{0:T(1024)S(1)}, u32[]{:S(2)}) copy-start(s32[2048]{0:T(1024)S(1)} %get-tuple-element.601) | copy-start | bytes 24580
  542.7 40.7 %all-to-all-start.3 = ((bf16[4,512,512]{1,2,0:T(8,128)(2,1)}), bf16[4,512,512]{1,2,0:T(8,128)(2,1)}, u32[]{:S(2)}, u32[]{:S(2)}) async-start(bf16[4,512,512]{1,2,0:T(8,128)(2,1)} %bitcast.388), calls=%async_computation.3 | async-start | bytes 4194304 | tf_op jit(solution)/shard_map/all_to_all | solution.py:237
  547.6 17.3 copy-start.39
  564.9 18.5 copy-start.72
  564.9 18.5 copy-start.79
  597.8 133.0 %copy-start.13 = (bf16[512,2048]{1,0:T(8,128)(2,1)}, bf16[512,2048]{1,0:T(8,128)(2,1)S(1)}, u32[]{:S(2)}) copy-start(bf16[512,2048]{1,0:T(8,128)(2,1)S(1)} %add_convert_fusion.2) | copy-start | bytes 6291460
  601.6 139.3 %copy-start.53 = (bf16[512,128]{1,0:T(8,128)(2,1)}, bf16[512,128]{1,0:T(8,128)(2,1)S(1)}, u32[]{:S(2)}) copy-start(bf16[512,128]{1,0:T(8,128)(2,1)S(1)} %fusion.98) | copy-start | bytes 393220
  699.0 31.7 %copy-start.33 = (bf16[2,5632,128]{2,1,0:T(8,128)(2,1)S(1)}, bf16[2,5632,128]{2,1,0:T(8,128)(2,1)}, u32[]{:S(2)}) copy-start(bf16[2,5632,128]{2,1,0:T(8,128)(2,1)} %param.39) | copy-start | bytes 8650756
  740.9 20.0 copy-start.34
  765.4 38.3 %copy-start.41 = (bf16[512,128]{1,0:T(8,128)(2,1)}, bf16[512,128]{1,0:T(8,128)(2,1)S(1)}, u32[]{:S(2)}) copy-start(bf16[512,128]{1,0:T(8,128)(2,1)S(1)} %fusion.110) | copy-start | bytes 393220
  771.5 32.2 %copy-start.56 = (f32[2048]{0:T(1024)S(1)}, f32[2048]{0:T(1024)}, u32[]{:S(2)}) copy-start(f32[2048]{0:T(1024)} %convert_element_type.204) | copy-start | bytes 24580
  771.5 32.2 %copy-start.60 = (f32[512]{0:T(512)S(1)}, f32[512]{0:T(512)}, u32[]{:S(2)}) copy-start(f32[512]{0:T(512)} %copy-done.59) | copy-start | bytes 6148
  771.5 32.2 %copy-start.64 = (f32[512]{0:T(512)S(1)}, f32[512]{0:T(512)}, u32[]{:S(2)}) copy-start(f32[512]{0:T(512)} %copy-done.63) | copy-start | bytes 6148
  803.7 10.5 slice-start.2
  822.1 29.2 %all-to-all-start.4 = ((bf16[512,4,512]{2,0,1:T(8,128)(2,1)}), bf16[512,4,512]{2,0,1:T(8,128)(2,1)S(1)}, u32[]{:S(2)}, u32[]{:S(2)}) async-start(bf16[512,4,512]{2,0,1:T(8,128)(2,1)} %bitcast.382), calls=%async_computation.4 | async-start | bytes 4194304 | tf_op jit(solution)/shard_map/all_to_all | solution.py:327
  1417.1 35.1 %all-to-all-start.6 = ((bf16[4,512,512]{1,2,0:T(8,128)(2,1)}), bf16[4,512,512]{1,2,0:T(8,128)(2,1)}, u32[]{:S(2)}, u32[]{:S(2)}) async-start(bf16[4,512,512]{1,2,0:T(8,128)(2,1)} %copy.109), calls=%async_computation.6 | async-start | bytes 4194304 | tf_op jit(solution)/shard_map/all_to_all | solution.py:372
  1421.7 216.2 %all-reduce.5.cloned.1.call-start = ((), (), s32[]{:S(2)}) async-start(), calls=%async_computation.16 | async-start | bytes 17301504
  1452.3 43.1 %all-to-all-start.5 = ((bf16[4,512,512]{1,2,0:T(8,128)(2,1)}), bf16[4,512,512]{1,2,0:T(8,128)(2,1)}, u32[]{:S(2)}, u32[]{:S(2)}) async-start(bf16[4,512,512]{1,2,0:T(8,128)(2,1)} %copy.108), calls=%async_computation.5 | async-start | bytes 4194304 | tf_op jit(solution)/shard_map/all_to_all | solution.py:371
  1462.0 37.2 %copy-start.73 = (s32[512]{0:T(512)S(1)}, s32[512]{0:T(512)}, u32[]{:S(2)}) copy-start(s32[512]{0:T(512)} %copy-done.71) | copy-start | bytes 6148
  1462.0 37.2 %copy-start.80 = (s32[128]{0:T(128)S(1)}, s32[128]{0:T(128)}, u32[]{:S(2)}) copy-start(s32[128]{0:T(128)} %copy-done.78) | copy-start | bytes 1540
  1495.3 35.1 %all-to-all-start.7 = ((bf16[4,512,512]{1,2,0:T(8,128)(2,1)}), bf16[4,512,512]{1,2,0:T(8,128)(2,1)S(1)}, u32[]{:S(2)}, u32[]{:S(2)}) async-start(bf16[4,512,512]{1,2,0:T(8,128)(2,1)} %copy.110), calls=%async_computation.7 | async-start | bytes 4194304 | tf_op jit(solution)/shard_map/all_to_all | solution.py:373
  1499.0 324.3 %reduce-scatter.5.cloned.1.call-start = ((), (), s32[]{:S(2)}) async-start(), calls=%async_computation.15 | async-start | bytes 8650752 | tf_op jit(solution)/shard_map/reduce_scatter | solution.py:409
  1503.9 27.8 %copy-start.48 = (bf16[512,128]{1,0:T(8,128)(2,1)S(1)}, bf16[512,128]{1,0:T(8,128)(2,1)}, u32[]{:S(2)}) copy-start(bf16[512,128]{1,0:T(8,128)(2,1)} %copy-done.47) | copy-start | bytes 393220
  1504.0 31.2 %copy-start.50 = (bf16[512,128]{1,0:T(8,128)(2,1)S(1)}, bf16[512,128]{1,0:T(8,128)(2,1)}, u32[]{:S(2)}) copy-start(bf16[512,128]{1,0:T(8,128)(2,1)} %copy-done.49) | copy-start | bytes 393220
  1549.2 460.6 %reduce-scatter.3.cloned.1.call-start = ((), (), s32[]{:S(2)}) async-start(), calls=%async_computation.14 | async-start | bytes 8650752 | tf_op jit(solution)/shard_map/reduce_scatter | solution.py:407
  1578.8 17.1 copy-start.6
  1634.9 376.6 %copy-start.1 = (bf16[256,6144]{1,0:T(8,128)(2,1)S(1)}, bf16[256,6144]{1,0:T(8,128)(2,1)}, u32[]{:S(2)}) copy-start(bf16[256,6144]{1,0:T(8,128)(2,1)} %param.29) | copy-start | bytes 9437188
  (54 other events, 286.4 us)
Sparse Core Ops, SparseCore 0:
  11.4 156.7 all-gather.4
  171.0 189.3 all-gather.10
  363.3 76.1 all-gather.6
  442.2 256.7 all-gather.8
  1444.0 192.7 all-reduce.4
  1638.9 184.3 reduce-scatter.4
  1825.6 184.1 reduce-scatter.2
